TPU v7x, 32 devices: a whole 2x2x4 slice. The times are simulated.
32 devices in a mesh: chan: 8 (over y, x, core), win: 4 (over z).
Axes of the slice: x: 2, y: 2, z: 4, core: 2. Of those that a mesh axis runs over, the one named last changes fastest.
Arguments:
- records: float32 [16, 1024, 256], P('win', 'chan'), may hold values from -180 to 180
- sources: int32 [32], replicated, may hold values from 0 to 255, as said below
Outputs:
- correlations: float32 [32, 256, 256], P('win', None, 'chan')
Inputs may be any that keep to these rules, and one draw needn't show every extreme that they name: `sources`: source s is one of the channels s * 8 to (s + 1) * 8 - 1; the first source is channel 0 and the last is channel 256 - 1.
All inputs are finite; a program needn't handle non-finite values.
Results may differ from a plain program's by a relative error of at most 0.00022.
Values sent between devices are 32-bit elements; how exact they have to be, the bound alone decides.
A program may use at most 64 MiB of HBM per device.

v0:
```python
import functools
import math

import jax
import jax.numpy as jnp
import numpy as np
from jax import lax
from jax.experimental import pallas as pl
from jax.experimental.pallas import tpu as pltpu
from jax.sharding import PartitionSpec as P

HIGHEST = lax.Precision.HIGHEST
AMPLITUDE_FLOOR = 0.25
WHITE_EPSILON = 1e-06


def fourier_table(length):
    freq_count = length // 2
    freqs = jnp.arange(freq_count, dtype=jnp.int32)[:, None]
    sample_index = jnp.arange(length, dtype=jnp.int32)[None, :]
    angles = (freqs * sample_index % length).astype(jnp.float32) * (2.0 * math.pi / length)
    return jnp.concatenate([jnp.cos(angles), -jnp.sin(angles)], axis=0)


def band_table(freq_count, reach):
    rows_index = jnp.arange(freq_count, dtype=jnp.int32)[:, None]
    cols_index = jnp.arange(freq_count, dtype=jnp.int32)[None, :]
    return (jnp.abs(rows_index - cols_index) <= reach).astype(jnp.float32)


def inverse_table(length, lag_count, first_bin, bin_count, factor):
    freqs = first_bin + jnp.arange(bin_count, dtype=jnp.int32)
    lag_index = jnp.arange(lag_count, dtype=jnp.int32) - lag_count // 2
    angles = (lag_index[:, None] * freqs[None, :] % length).astype(jnp.float32) * (
        2.0 * math.pi / length
    )
    weights = jnp.where(freqs == 0, 1.0, 2.0).astype(jnp.float32)[None, :] * factor
    return jnp.concatenate([weights * jnp.cos(angles), -weights * jnp.sin(angles)], axis=1)


def running_level(padded, time_count, window_span):
    window_total = padded.shape[0]
    chans = padded.shape[2]
    running = jnp.concatenate(
        [jnp.zeros((window_total, 1, chans), jnp.float32), jnp.cumsum(jnp.abs(padded), axis=1)],
        axis=1,
    )
    return (running[:, window_span:] - running[:, :time_count]) / window_span


def local(records, sources):
    chan_count = lax.axis_size("chan")
    local_windows, local_time, all_channels = records.shape
    length = local_time * chan_count
    freq_count = length // 2
    chan_width = all_channels // chan_count
    half_width = min(16, local_time)
    smooth_reach = length // 32
    window_span = 2 * half_width + 1
    lag_count = length // 4
    forward = fourier_table(length)
    band_matrix = band_table(freq_count, smooth_reach)
    pieces = lax.all_to_all(records, "chan", split_axis=2, concat_axis=1, tiled=True)
    padded = jnp.pad(pieces, ((0, 0), (half_width, half_width), (0, 0)))
    amplitude = running_level(padded, length, window_span)
    whiten_pieces = pieces / jnp.maximum(amplitude, AMPLITUDE_FLOOR)
    spectrum = jnp.einsum("kt,wtc->wkc", forward, whiten_pieces, precision=HIGHEST)
    real_part = spectrum[:, :freq_count]
    imag_part = spectrum[:, freq_count:]
    magnitude = jnp.sqrt(real_part * real_part + imag_part * imag_part)
    smoothed = (
        jnp.einsum("jk,wkc->wjc", band_matrix, magnitude, precision=HIGHEST)
        / (2 * smooth_reach + 1)
        + WHITE_EPSILON
    )
    whitened = jnp.stack([real_part / smoothed, imag_part / smoothed], axis=1)
    band_data = lax.all_to_all(whitened, "win", split_axis=2, concat_axis=0, tiled=True)
    total_windows = band_data.shape[0]
    band_count = band_data.shape[2]
    source_count = sources.shape[0]
    chan_index = lax.axis_index("chan")
    channel_ids = jnp.arange(chan_width, dtype=jnp.int32)
    per_device = source_count // chan_count
    owned_local = (
        lax.dynamic_slice_in_dim(sources, chan_index * per_device, per_device)
        - chan_index * chan_width
    )
    selector = (owned_local[:, None] == channel_ids[None, :]).astype(jnp.float32)
    chosen = jnp.einsum("sc,wafc->wafs", selector, band_data, precision=HIGHEST)
    spectra = lax.all_gather(chosen, "chan", axis=3, tiled=True)
    source_real = spectra[:, 0]
    source_imag = spectra[:, 1]
    white_real = band_data[:, 0]
    white_imag = band_data[:, 1]
    cross_real = jnp.einsum(
        "wfs,wfc->fsc", source_real, white_real, precision=HIGHEST
    ) + jnp.einsum("wfs,wfc->fsc", source_imag, white_imag, precision=HIGHEST)
    cross_imag = jnp.einsum(
        "wfs,wfc->fsc", source_real, white_imag, precision=HIGHEST
    ) - jnp.einsum("wfs,wfc->fsc", source_imag, white_real, precision=HIGHEST)
    stacked = jnp.stack([cross_real, cross_imag])
    factor = 1.0 / math.sqrt(total_windows * freq_count)
    band_start = lax.axis_index("win") * band_count
    band_table_part = inverse_table(length, lag_count, band_start, band_count, factor).reshape(
        lag_count, 2, band_count
    )
    return lax.psum_scatter(
        jnp.einsum("tak,aksc->stc", band_table_part, stacked, precision=HIGHEST),
        "win",
        scatter_dimension=0,
        tiled=True,
    )


LANES = 128
PIECES = 4
BF16 = jnp.bfloat16
MESH = pl.DeviceIdType.MESH


def bin_order(freq_count):
    per = freq_count // 8
    pairs = ((0, 4), (1, 7), (2, 6), (3, 5))
    return np.concatenate([8 * np.arange(per) + m for pair in pairs for m in pair])


def split_table(table):
    high = table.astype(np.float32).astype(BF16)
    low = (table - high.astype(np.float64)).astype(np.float32).astype(BF16)
    return np.stack([high, low])


def forward_blocks(length, time):
    per = length // 16
    rows = np.arange(time)[:, None]
    blocks = []
    for first, second in ((0, 4), (1, 7), (2, 6), (3, 5)):
        angle1 = 2 * np.pi * ((8 * np.arange(per) + first)[None, :] * rows % length) / length
        angle2 = 2 * np.pi * ((8 * np.arange(per) + second)[None, :] * rows % length) / length
        c1, s1, c2, s2 = np.cos(angle1), np.sin(angle1), np.cos(angle2), np.sin(angle2)
        if first == 0:
            zero = np.zeros_like(c1)
            top = np.concatenate([c1, zero, -s1, zero], axis=1)
            low = np.concatenate([zero, c2, zero, -s2], axis=1)
        else:
            top = np.concatenate([c1, c2, -s1, -s2], axis=1)
            low = np.concatenate([s1, -s2, c1, -c2], axis=1)
        blocks.append(np.concatenate([top, low], axis=0))
    return split_table(np.stack(blocks))


def smooth_table(freq_count, reach):
    order = bin_order(freq_count)
    return (np.abs(order[:, None] - order[None, :]) <= reach).astype(np.float32).astype(BF16)


def lag_table(length, lag_count, factor):
    bins = bin_order(length // 2)[:, None]
    lags = (np.arange(lag_count) - lag_count // 2)[None, :]
    angle = 2 * np.pi * (bins * lags % length) / length
    weight = np.where(bins == 0, 1.0, 2.0) * factor
    return split_table(np.concatenate([weight * np.cos(angle), -weight * np.sin(angle)], axis=0))


def halves(value):
    high = value.astype(BF16)
    return high, (value - high.astype(jnp.float32)).astype(BF16)


def dot(a, b):
    return jnp.dot(a, b, preferred_element_type=jnp.float32)


def fused_kernel(
    half_width, smooth_reach, chan_count, win_count, per_device,
    src_ref, rec_hbm, fwd_hbm, band_hbm, lag_hbm, out_ref,
    rec, xt, recv, nrm, yh, yl, mh, ml, wr, wi, gs, ch, cl, part, from_left, from_right,
    fwd, band, lag,
    rec_sem, tab_sem, a_send, a_recv, g_send, g_recv, r_send, left_sem, right_sem,
):
    me = lax.axis_index("chan")
    row = lax.axis_index("win")
    windows, time, _ = rec.shape
    rows = recv.shape[1]
    width = rows // windows
    freq = wr.shape[1]
    tiles = freq // LANES
    core, x, y = lax.rem(me, 2), lax.rem(me // 2, 2), me // 4
    upper = row // 2
    inner = lax.rem(row + upper, 2)

    def flipped(d):
        bits = ((core, 1), (x, 2), (y, 4))
        return me + sum(b * (1 - 2 * bit) for bit, b in bits if d & b)

    barrier = pltpu.get_barrier_semaphore()
    for d in range(1, chan_count):
        pl.semaphore_signal(barrier, inc=1, device_id={"chan": flipped(d)}, device_id_type=MESH)

    @pl.when(row > 0)
    def _():
        pl.semaphore_signal(barrier, inc=1, device_id={"win": row - 1}, device_id_type=MESH)

    @pl.when(row < win_count - 1)
    def _():
        pl.semaphore_signal(barrier, inc=1, device_id={"win": row + 1}, device_id_type=MESH)

    loads = [
        pltpu.make_async_copy(rec_hbm.at[w], rec.at[w], rec_sem.at[w]) for w in range(windows)
    ]
    tables = [
        pltpu.make_async_copy(hbm, vmem, tab_sem.at[i])
        for i, (hbm, vmem) in enumerate(((fwd_hbm, fwd), (band_hbm, band), (lag_hbm, lag)))
    ]
    for copy in loads + tables:
        copy.start()
    for w in range(windows):
        loads[w].wait()
        for h in range(rec.shape[2] // LANES):
            tile = rec[w, :, h * LANES : (h + 1) * LANES].T
            for i in range(LANES // width):
                xt[h * (LANES // width) + i, w * width : (w + 1) * width, :] = tile[
                    i * width : (i + 1) * width
                ]

    @pl.when(inner == 0)
    def _():
        pl.semaphore_wait(barrier, chan_count)

    @pl.when(inner == 1)
    def _():
        pl.semaphore_wait(barrier, chan_count + 1)

    exchange = []
    for d in (6, 7, 4, 5, 2, 3, 1):
        peer = flipped(d)
        copy = pltpu.make_async_remote_copy(
            src_ref=xt.at[peer], dst_ref=recv.at[me], send_sem=a_send.at[d], recv_sem=a_recv.at[d],
            device_id={"chan": peer}, device_id_type=MESH,
        )
        copy.start()
        exchange.append(copy)
    recv[me] = xt[me]
    near_row = lax.broadcasted_iota(jnp.int32, (3 * time, time), 0) - time
    near_col = lax.broadcasted_iota(jnp.int32, (3 * time, time), 1)
    near = (jnp.abs(near_row - near_col) <= half_width).astype(jnp.float32).astype(BF16)
    for copy in exchange:
        copy.wait_recv()

    for i in range(8):
        lo, hi = max(i - 1, 0), min(i + 1, 7)
        level = jnp.zeros((rows, time), jnp.float32)
        for j in range(lo, hi + 1):
            high, low = halves(jnp.abs(recv[j]))
            weights = near[(j - i + 1) * time : (j - i + 2) * time]
            level = level + (dot(high, weights) + dot(low, weights))
        level = level * (1.0 / (2 * half_width + 1))
        nrm[i] = recv[i] / jnp.maximum(level, AMPLITUDE_FLOOR)

    root = math.sqrt(0.5)

    def butterfly(block, _):
        at = pl.ds(pl.multiple_of(block * width, width), width)
        n = [nrm[i, at, :] for i in range(8)]
        a = [n[i] + n[i + 4] for i in range(4)]
        b = [n[i] - n[i + 4] for i in range(4)]
        even, odd = a[0] + a[2], a[1] + a[3]
        diff, total = root * (b[1] - b[3]), root * (b[1] + b[3])
        pairs = (
            (even + odd, even - odd),
            (b[0] + diff, -(b[2] + total)),
            (a[0] - a[2], a[3] - a[1]),
            (b[0] - diff, b[2] - total),
        )
        for g, pair in enumerate(pairs):
            for side, value in enumerate(pair):
                high, low = halves(value)
                yh[g, at, side * time : (side + 1) * time] = high
                yl[g, at, side * time : (side + 1) * time] = low
        return 0

    lax.fori_loop(0, windows, butterfly, 0)
    tables[0].wait()
    for g in range(4):
        at = slice(g * LANES, (g + 1) * LANES)
        both = dot(yh[g], fwd[0, g]) + dot(yl[g], fwd[0, g]) + dot(yh[g], fwd[1, g])
        real, imag = both[:, :LANES], both[:, LANES:]
        wr[:, at] = real
        wi[:, at] = imag
        high, low = halves(jnp.sqrt(real * real + imag * imag))
        mh[:, at] = high
        ml[:, at] = low
    tables[1].wait()
    for g in range(freq // 256):
        at = slice(g * 256, (g + 1) * 256)
        smoothed = (dot(mh[...], band[:, at]) + dot(ml[...], band[:, at])) / (
            2 * smooth_reach + 1
        ) + WHITE_EPSILON
        wr[:, at] = wr[:, at] / smoothed
        wi[:, at] = wi[:, at] / smoothed

    for i in range(per_device):
        owned = lax.rem(src_ref[me * per_device + i], width)
        for w in range(windows):
            at = 2 * (windows * i + w)
            gs[me, at : at + 1, :] = wr[pl.ds(w * width + owned, 1), :]
            gs[me, at + 1 : at + 2, :] = wi[pl.ds(w * width + owned, 1), :]
    def passing(block, target):
        slot = gs.at[flipped(block)]
        return pltpu.make_async_remote_copy(
            src_ref=slot, dst_ref=slot, send_sem=g_send.at[block ^ target],
            recv_sem=g_recv.at[block ^ target], device_id={"chan": flipped(target)},
            device_id_type=MESH,
        )

    gather = {b ^ t: passing(b, t) for b, t in ((0, 4), (0, 2), (0, 1), (4, 1), (4, 2), (2, 1), (6, 1))}
    for d in (4, 2, 1):
        gather[d].start()
    tables[2].wait()

    away = (1 - upper) * (1 - y) + upper * y

    def chunk_of(q):
        p, k = q // 2, lax.rem(q, 2)
        dx, late = lax.rem(p, 2), p // 2
        dy = away + late * (1 - 2 * away)
        owner = 2 * (y + dy * (1 - 2 * y)) + x + dx * (1 - 2 * x)
        return owner, core + k * (1 - 2 * core), 4 * dy + 2 * dx + k

    def compute(owner, half):
        device = owner * 2 + half
        for t in range(tiles):
            at = slice(t * LANES, (t + 1) * LANES)
            white = [
                (wr[w * width : (w + 1) * width, at], wi[w * width : (w + 1) * width, at])
                for w in range(windows)
            ]
            for i in range(per_device):
                real = imag = None
                for w in range(windows):
                    line = 2 * (windows * i + w)
                    sr = gs[device, line : line + 1, at]
                    si = gs[device, line + 1 : line + 2, at]
                    r = sr * white[w][0] + si * white[w][1]
                    m = sr * white[w][1] - si * white[w][0]
                    real = r if real is None else real + r
                    imag = m if imag is None else imag + m
                for side, value in enumerate((real, imag)):
                    high, low = halves(value)
                    col = side * freq + t * LANES
                    ch[i * width : (i + 1) * width, col : col + LANES] = high
                    cl[i * width : (i + 1) * width, col : col + LANES] = low
        part[device] = dot(ch[...], lag[0]) + dot(cl[...], lag[0]) + dot(ch[...], lag[1])

    piece = part.shape[1] // PIECES

    def hop(slot, k, landing, sem, target):
        at = pl.ds(k * piece, piece)
        return pltpu.make_async_remote_copy(
            src_ref=part.at[slot, at], dst_ref=landing.at[slot, at],
            send_sem=r_send.at[slot * PIECES + k], recv_sem=sem.at[slot * PIECES + k],
            device_id={"win": target}, device_id_type=MESH,
        )

    def finish(owner, half):
        slot = owner * 2 + half

        @pl.when(owner > row)
        def _():
            for k in range(PIECES):
                right = hop(slot, k, from_left, left_sem, row + 1)

                @pl.when(row > 0)
                def _():
                    right.wait_recv()
                    at = slice(k * piece, (k + 1) * piece)
                    part[slot, at] = part[slot, at] + from_left[slot, at]

                right.start()

        @pl.when(owner < row)
        def _():
            for k in range(PIECES):
                left = hop(slot, k, from_right, right_sem, row - 1)

                @pl.when(row < win_count - 1)
                def _():
                    left.wait_recv()
                    at = slice(k * piece, (k + 1) * piece)
                    part[slot, at] = part[slot, at] + from_right[slot, at]

                left.start()

    def step(q, _):
        owner, half, d = chunk_of(q)

        @pl.when(q == 2 * (1 - away))
        def _():
            gather[4].wait_recv()
            gather[6].start()
            gather[5].start()
            gather[2].wait_recv()
            gather[3].start()

        @pl.when(q == 2 * (2 - away))
        def _():
            gather[6].wait_recv()
            gather[7].start()

        @pl.when(lax.rem(q, 2) == 1)
        def _():
            pltpu.make_async_remote_copy(
                src_ref=gs.at[me], dst_ref=gs.at[me], send_sem=g_send.at[d], recv_sem=g_recv.at[d],
                device_id={"chan": lax.rem(me + 1, chan_count)}, device_id_type=MESH,
            ).wait_recv()

        compute(owner, half)

        @pl.when(inner == 0)
        def _():
            finish(owner, half)

        @pl.when((inner == 1) & (q >= 2) & (q < 4))
        def _():
            first, side, _ = chunk_of(q - 2)
            finish(first, side)

        return 0

    chunks = 2 * win_count
    lax.fori_loop(0, chunks, step, 0)

    back = 3 * upper

    def finish_back(when):
        @pl.when((inner == 1) & (when == 0))
        def _():
            for k in range(2):
                finish(back, core + k * (1 - 2 * core))

    parity = x + upper * (1 - 2 * x)
    finish_back(parity)

    @pl.when(inner == 1)
    def _():
        for q in (2, 3):
            owner, half, _ = chunk_of(q)
            finish(owner, half)

    finish_back(1 - parity)

    block = part.shape[1]
    for k in range(2):
        half = core + k * (1 - 2 * core)
        slot = row * 2 + half
        at = pl.ds(pl.multiple_of(half * block, block), block)
        out_ref[at, :] = part[slot]

        @pl.when(row < win_count - 1)
        def _():
            for j in range(PIECES):
                hop(slot, j, from_right, right_sem, row + 1).wait_recv()
            out_ref[at, :] += from_right[slot]

        @pl.when(row > 0)
        def _():
            for j in range(PIECES):
                hop(slot, j, from_left, left_sem, row - 1).wait_recv()
            out_ref[at, :] += from_left[slot]

    for copy in exchange + list(gather.values()):
        copy.wait_send()
    for slot in range(chunks):
        @pl.when(row != slot // 2)
        def _():
            for k in range(PIECES):
                hop(slot, k, from_left, left_sem, lax.rem(row + 1, win_count)).wait_send()


def fused(records, sources):
    chan_count, win_count = lax.axis_size("chan"), lax.axis_size("win")
    windows, time, channels = records.shape
    length = time * chan_count
    freq = length // 2
    width = channels // chan_count
    rows = windows * width
    source_count = sources.shape[0]
    lag_count = length // 4
    reach = length // 32
    half_width = min(16, time)
    owned = source_count // win_count
    factor = 1.0 / math.sqrt(windows * win_count * freq)
    fwd = forward_blocks(length, time)
    band = smooth_table(freq, reach)
    lag = lag_table(length, lag_count, factor)
    f32 = jnp.float32
    block = owned * width
    half = block // 2
    per_device = source_count // chan_count
    vmem = pl.BlockSpec(memory_space=pltpu.VMEM)
    hbm = pl.BlockSpec(memory_space=pltpu.HBM)
    out = pl.pallas_call(
        functools.partial(fused_kernel, half_width, reach, chan_count, win_count, per_device),
        out_shape=jax.ShapeDtypeStruct((block, lag_count), f32),
        in_specs=[pl.BlockSpec(memory_space=pltpu.SMEM), hbm, hbm, hbm, hbm],
        out_specs=vmem,
        scratch_shapes=[
            pltpu.VMEM(records.shape, f32),
            pltpu.VMEM((chan_count, rows, time), f32),
            pltpu.VMEM((chan_count, rows, time), f32),
            pltpu.VMEM((chan_count, rows, time), f32),
            pltpu.VMEM((4, rows, 2 * time), BF16),
            pltpu.VMEM((4, rows, 2 * time), BF16),
            pltpu.VMEM((rows, freq), BF16),
            pltpu.VMEM((rows, freq), BF16),
            pltpu.VMEM((rows, freq), f32),
            pltpu.VMEM((rows, freq), f32),
            pltpu.VMEM((chan_count, 2 * windows * per_device, freq), f32),
            pltpu.VMEM((half, 2 * freq), BF16),
            pltpu.VMEM((half, 2 * freq), BF16),
            pltpu.VMEM((2 * win_count, half, lag_count), f32),
            pltpu.VMEM((2 * win_count, half, lag_count), f32),
            pltpu.VMEM((2 * win_count, half, lag_count), f32),
            pltpu.VMEM(fwd.shape, BF16),
            pltpu.VMEM(band.shape, BF16),
            pltpu.VMEM(lag.shape, BF16),
            pltpu.SemaphoreType.DMA((windows,)),
            pltpu.SemaphoreType.DMA((3,)),
            pltpu.SemaphoreType.DMA((chan_count,)),
            pltpu.SemaphoreType.DMA((chan_count,)),
            pltpu.SemaphoreType.DMA((chan_count,)),
            pltpu.SemaphoreType.DMA((chan_count,)),
            pltpu.SemaphoreType.DMA((2 * win_count * PIECES,)),
            pltpu.SemaphoreType.DMA((2 * win_count * PIECES,)),
            pltpu.SemaphoreType.DMA((2 * win_count * PIECES,)),
        ],
        compiler_params=pltpu.CompilerParams(
            collective_id=0, has_side_effects=True, vmem_limit_bytes=66_400_000
        ),
        name="interferometry",
    )(sources, records, jnp.asarray(fwd), jnp.asarray(band), jnp.asarray(lag))
    return out.reshape(owned, width, lag_count).transpose(0, 2, 1)


def fits(records, sources):
    chan_count, win_count = lax.axis_size("chan"), lax.axis_size("win")
    time, channels = records.shape[1:]
    width = channels // chan_count
    return (
        time == LANES and chan_count == 8 and win_count == 4 and channels % LANES == 0
        and LANES % width == 0 and width % 16 == 0 and sources.shape[0] % chan_count == 0
    )


def body(records, sources):
    return fused(records, sources) if fits(records, sources) else local(records, sources)


def solution(mesh):
    placed = (P("win", "chan", None), P())
    return jax.shard_map(
        body, mesh=mesh, in_specs=placed, out_specs=P("win", None, "chan"), check_vma=False
    )
```

profile of v0, /device:TPU:6, one launch (start us, length us, event | category | flops | bytes accessed | tf_op | source)
XLA Modules:
  0.0 40.4 jit_solution(11144432572438474237)
XLA Ops:
  0.0 38.7 %interferometry.1 = f32[256,256]{1,0:T(8,128)} custom-call(s32[32]{0:T(128)} %src_ref.1, f32[4,128,256]{2,1,0:T(8,128)} %rec_hbm.1, bf16[2,4,256,256]{3,2,1,0:T(8,128)(2,1)} %constant.6.clone.fwd_hbm, bf16[512,512]{1,0:T(8,128)(2,1)} %constant.7.clone.band_hbm, bf16[2,1024,256]{2,1,0:T(8,128)(2,1)} %constant.8.clone.lag_hbm), custom_call_target="tpu_custom_call" | custom-call | tf_op jit(solution)/shard_map/interferometry/pallas_call | solution.py:502
  38.7 1.7 %copy.7 = f32[8,256,32]{1,2,0:T(8,128)} copy(f32[8,256,32]{1,2,0:T(8,128)} %bitcast.3) | data formatting | bytes 524288
where the time goes:
time: 40.6 us; the launch traced here: 40.4 us
  Pallas kernels  38.7 us (95%)
  local copies, waits for them, and re-layouts  1.67 us (4%)
    pallas_call x1, Pallas kernels, fused(): pl.pallas_call(functools.partial(fused_kernel, half_width, reach, chan_co...  38.7 us
    unnamed x1, local copies, waits for them, and re-layouts  1.67 us

commit v1 on v0

v1 whole, which is shorter than its diff:
```python
import functools
import math

import jax
import jax.numpy as jnp
import numpy as np
from jax import lax
from jax.experimental import pallas as pl
from jax.experimental.pallas import tpu as pltpu
from jax.sharding import PartitionSpec as P

HIGHEST = lax.Precision.HIGHEST
AMPLITUDE_FLOOR = 0.25
WHITE_EPSILON = 1e-06


def fourier_table(length):
    freq_count = length // 2
    freqs = jnp.arange(freq_count, dtype=jnp.int32)[:, None]
    sample_index = jnp.arange(length, dtype=jnp.int32)[None, :]
    angles = (freqs * sample_index % length).astype(jnp.float32) * (2.0 * math.pi / length)
    return jnp.concatenate([jnp.cos(angles), -jnp.sin(angles)], axis=0)


def band_table(freq_count, reach):
    rows_index = jnp.arange(freq_count, dtype=jnp.int32)[:, None]
    cols_index = jnp.arange(freq_count, dtype=jnp.int32)[None, :]
    return (jnp.abs(rows_index - cols_index) <= reach).astype(jnp.float32)


def inverse_table(length, lag_count, first_bin, bin_count, factor):
    freqs = first_bin + jnp.arange(bin_count, dtype=jnp.int32)
    lag_index = jnp.arange(lag_count, dtype=jnp.int32) - lag_count // 2
    angles = (lag_index[:, None] * freqs[None, :] % length).astype(jnp.float32) * (
        2.0 * math.pi / length
    )
    weights = jnp.where(freqs == 0, 1.0, 2.0).astype(jnp.float32)[None, :] * factor
    return jnp.concatenate([weights * jnp.cos(angles), -weights * jnp.sin(angles)], axis=1)


def running_level(padded, time_count, window_span):
    window_total = padded.shape[0]
    chans = padded.shape[2]
    running = jnp.concatenate(
        [jnp.zeros((window_total, 1, chans), jnp.float32), jnp.cumsum(jnp.abs(padded), axis=1)],
        axis=1,
    )
    return (running[:, window_span:] - running[:, :time_count]) / window_span


def local(records, sources):
    chan_count = lax.axis_size("chan")
    local_windows, local_time, all_channels = records.shape
    length = local_time * chan_count
    freq_count = length // 2
    chan_width = all_channels // chan_count
    half_width = min(16, local_time)
    smooth_reach = length // 32
    window_span = 2 * half_width + 1
    lag_count = length // 4
    forward = fourier_table(length)
    band_matrix = band_table(freq_count, smooth_reach)
    pieces = lax.all_to_all(records, "chan", split_axis=2, concat_axis=1, tiled=True)
    padded = jnp.pad(pieces, ((0, 0), (half_width, half_width), (0, 0)))
    amplitude = running_level(padded, length, window_span)
    whiten_pieces = pieces / jnp.maximum(amplitude, AMPLITUDE_FLOOR)
    spectrum = jnp.einsum("kt,wtc->wkc", forward, whiten_pieces, precision=HIGHEST)
    real_part = spectrum[:, :freq_count]
    imag_part = spectrum[:, freq_count:]
    magnitude = jnp.sqrt(real_part * real_part + imag_part * imag_part)
    smoothed = (
        jnp.einsum("jk,wkc->wjc", band_matrix, magnitude, precision=HIGHEST)
        / (2 * smooth_reach + 1)
        + WHITE_EPSILON
    )
    whitened = jnp.stack([real_part / smoothed, imag_part / smoothed], axis=1)
    band_data = lax.all_to_all(whitened, "win", split_axis=2, concat_axis=0, tiled=True)
    total_windows = band_data.shape[0]
    band_count = band_data.shape[2]
    source_count = sources.shape[0]
    chan_index = lax.axis_index("chan")
    channel_ids = jnp.arange(chan_width, dtype=jnp.int32)
    per_device = source_count // chan_count
    owned_local = (
        lax.dynamic_slice_in_dim(sources, chan_index * per_device, per_device)
        - chan_index * chan_width
    )
    selector = (owned_local[:, None] == channel_ids[None, :]).astype(jnp.float32)
    chosen = jnp.einsum("sc,wafc->wafs", selector, band_data, precision=HIGHEST)
    spectra = lax.all_gather(chosen, "chan", axis=3, tiled=True)
    source_real = spectra[:, 0]
    source_imag = spectra[:, 1]
    white_real = band_data[:, 0]
    white_imag = band_data[:, 1]
    cross_real = jnp.einsum(
        "wfs,wfc->fsc", source_real, white_real, precision=HIGHEST
    ) + jnp.einsum("wfs,wfc->fsc", source_imag, white_imag, precision=HIGHEST)
    cross_imag = jnp.einsum(
        "wfs,wfc->fsc", source_real, white_imag, precision=HIGHEST
    ) - jnp.einsum("wfs,wfc->fsc", source_imag, white_real, precision=HIGHEST)
    stacked = jnp.stack([cross_real, cross_imag])
    factor = 1.0 / math.sqrt(total_windows * freq_count)
    band_start = lax.axis_index("win") * band_count
    band_table_part = inverse_table(length, lag_count, band_start, band_count, factor).reshape(
        lag_count, 2, band_count
    )
    return lax.psum_scatter(
        jnp.einsum("tak,aksc->stc", band_table_part, stacked, precision=HIGHEST),
        "win",
        scatter_dimension=0,
        tiled=True,
    )


LANES = 128
STAGES = 2
BF16 = jnp.bfloat16
F32 = jnp.float32
MESH = pl.DeviceIdType.MESH


def bin_order(freq_count):
    per = freq_count // 8
    pairs = ((0, 4), (1, 7), (2, 6), (3, 5))
    return np.concatenate([8 * np.arange(per) + m for pair in pairs for m in pair])


def split_table(table):
    high = table.astype(np.float32).astype(BF16)
    low = (table - high.astype(np.float64)).astype(np.float32).astype(BF16)
    return np.stack([high, low])


def forward_blocks(length, time):
    per = length // 16
    rows = np.arange(time)[:, None]
    blocks = []
    for first, second in ((0, 4), (1, 7), (2, 6), (3, 5)):
        angle1 = 2 * np.pi * ((8 * np.arange(per) + first)[None, :] * rows % length) / length
        angle2 = 2 * np.pi * ((8 * np.arange(per) + second)[None, :] * rows % length) / length
        c1, s1, c2, s2 = np.cos(angle1), np.sin(angle1), np.cos(angle2), np.sin(angle2)
        if first == 0:
            zero = np.zeros_like(c1)
            top = np.concatenate([c1, zero, -s1, zero], axis=1)
            low = np.concatenate([zero, c2, zero, -s2], axis=1)
        else:
            top = np.concatenate([c1, c2, -s1, -s2], axis=1)
            low = np.concatenate([s1, -s2, c1, -c2], axis=1)
        blocks.append(np.concatenate([top, low], axis=0))
    return split_table(np.stack(blocks))


def smooth_table(freq_count, reach):
    order = bin_order(freq_count)
    return (np.abs(order[:, None] - order[None, :]) <= reach).astype(np.float32).astype(BF16)


def lag_table(length, lag_count, factor):
    bins = bin_order(length // 2)[:, None]
    lags = (np.arange(lag_count) - lag_count // 2)[None, :]
    angle = 2 * np.pi * (bins * lags % length) / length
    weight = np.where(bins == 0, 1.0, 2.0) * factor
    return split_table(np.concatenate([weight * np.cos(angle), -weight * np.sin(angle)], axis=0))


def halves(value):
    high = value.astype(BF16)
    return high, (value - high.astype(F32)).astype(BF16)


def stacked(value):
    return jnp.concatenate(halves(value), axis=0)


def dot(a, b):
    return jnp.dot(a, b, preferred_element_type=F32)


def folded(product):
    half = product.shape[0] // 2
    return product[:half] + product[half:]


def fused_kernel(
    half_width, smooth_reach, chan_count, win_count,
    src_hbm, rec_hbm, fwd_hbm, band_hbm, lag_hbm, out_ref,
    src_ref, rec, xt, recv, nrm, yy, fr, fi, mm, wr, wi, gs, cc, part, land,
    fwd, band, lag,
    rec_sem, tab_sem, a_send, a_recv, g_send, g_recv, r_send, r_recv,
):
    me = lax.axis_index("chan")
    row = lax.axis_index("win")
    windows, time, _ = rec.shape
    sets = 2 * windows
    group = xt.shape[2] // windows
    rows = sets * group
    width = STAGES * group
    freq = wr.shape[1]
    tiles = freq // LANES
    core, x, y = lax.rem(me, 2), lax.rem(me // 2, 2), me // 4
    upper, side = row // 2, lax.rem(row, 2)
    place = 2 * side + y
    far = (1 - upper, upper)
    column = [4 * far[s] + lax.rem(me, 4) for s in range(STAGES)]

    def flip(bit, by):
        return bit + by * (1 - 2 * bit)

    def masked(mask):
        dx, dy, z = mask >> 1 & 1, mask >> 2 & 1, mask >> 3
        chan = 4 * flip(y, dy) + 2 * flip(x, dx) + flip(core, mask & 1)
        return chan, row + z * (1 - 2 * side)

    def slot_of(chan, win):
        return lax.rem(win, 2) * chan_count + chan

    mine = slot_of(me, row)
    loads = [
        pltpu.make_async_copy(rec_hbm.at[w], rec.at[w], rec_sem.at[w]) for w in range(windows)
    ]
    tables = [
        pltpu.make_async_copy(hbm, vmem, tab_sem.at[i])
        for i, (hbm, vmem) in enumerate(
            ((fwd_hbm, fwd), (band_hbm, band), (lag_hbm, lag), (src_hbm, src_ref))
        )
    ]
    for copy in loads:
        copy.start()
    barrier = pltpu.get_barrier_semaphore()
    for mask in range(1, 2 * chan_count):
        chan, win = masked(mask)
        pl.semaphore_signal(
            barrier, inc=1, device_id={"chan": chan, "win": win}, device_id_type=MESH
        )
    for s in range(STAGES):
        for k in range(2):
            pl.semaphore_signal(
                barrier, inc=1, device_id={"chan": column[s], "win": 2 * (1 - upper) + k},
                device_id_type=MESH,
            )

    for copy in tables:
        copy.start()
    for w in range(windows):
        loads[w].wait()
        for h in range(2):
            tile = rec[w, :, h * LANES : (h + 1) * LANES].T
            for i in range(LANES // group):
                slot = i % 4 // 2 * chan_count + i % 2 * 4 + i // 4
                xt[h, slot, w * group : (w + 1) * group] = tile[i * group : (i + 1) * group]

    pl.semaphore_wait(barrier, 2 * chan_count - 1 + 2 * STAGES)

    for s in range(STAGES):
        for mask in (14, 15, 12, 13, 10, 11, 6, 7, 8, 9, 4, 5, 2, 3, 1):
            chan, win = masked(mask)
            pltpu.make_async_remote_copy(
                src_ref=xt.at[far[s], slot_of(chan, win)], dst_ref=recv.at[s, me, side],
                send_sem=a_send.at[s], recv_sem=a_recv.at[s],
                device_id={"chan": chan, "win": win}, device_id_type=MESH,
            ).start()
        pltpu.make_async_copy(xt.at[far[s], mine], recv.at[s, me, side], a_recv.at[s]).start()
    near_row = lax.broadcasted_iota(jnp.int32, (3 * time, time), 0) - time
    near_col = lax.broadcasted_iota(jnp.int32, (3 * time, time), 1)
    near = (jnp.abs(near_row - near_col) <= half_width).astype(F32).astype(BF16)
    root = math.sqrt(0.5)

    def settle(ref, sem):
        pltpu.make_async_copy(ref, ref, sem).wait()

    def normalise(s):
        for i in range(8):
            level = jnp.zeros((rows, time), F32)
            for j in range(max(i - 1, 0), min(i + 1, 7) + 1):
                both = stacked(jnp.abs(recv[s, j].reshape(rows, time)))
                level = level + folded(dot(both, near[(j - i + 1) * time : (j - i + 2) * time]))
            level = level * (1.0 / (2 * half_width + 1))
            nrm[i] = recv[s, i].reshape(rows, time) / jnp.maximum(level, AMPLITUDE_FLOOR)

    def butterfly(block, _):
        at = pl.ds(pl.multiple_of(block * 16, 16), 16)
        low_at = pl.ds(pl.multiple_of(rows + block * 16, 16), 16)
        n = [nrm[i, at, :] for i in range(8)]
        a = [n[i] + n[i + 4] for i in range(4)]
        b = [n[i] - n[i + 4] for i in range(4)]
        even, odd = a[0] + a[2], a[1] + a[3]
        diff, total = root * (b[1] - b[3]), root * (b[1] + b[3])
        pairs = (
            (even + odd, even - odd),
            (b[0] + diff, -(b[2] + total)),
            (a[0] - a[2], a[3] - a[1]),
            (b[0] - diff, b[2] - total),
        )
        for g, pair in enumerate(pairs):
            for k, value in enumerate(pair):
                high, low = halves(value)
                yy[g, at, k * time : (k + 1) * time] = high
                yy[g, low_at, k * time : (k + 1) * time] = low
        return 0

    def transform(s):
        lax.fori_loop(0, rows // 16, butterfly, 0)
        if s == 0:
            tables[0].wait()
        for g in range(4):
            at = slice(g * LANES, (g + 1) * LANES)
            both = folded(dot(yy[g], fwd[0, g])) + dot(yy[g, :rows], fwd[1, g])
            real, imag = both[:, :LANES], both[:, LANES:]
            fr[:, at] = real
            fi[:, at] = imag
            mm[:, at] = stacked(jnp.sqrt(real * real + imag * imag))

    def whiten(s):
        if s == 0:
            tables[1].wait()
        for g in range(freq // 256):
            at = slice(g * 256, (g + 1) * 256)
            smoothed = folded(dot(mm[...], band[:, at])) / (2 * smooth_reach + 1) + WHITE_EPSILON
            inverse = 1.0 / smoothed
            real, imag = fr[:, at] * inverse, fi[:, at] * inverse
            for w in range(sets):
                to = slice(w * width + s * group, w * width + (s + 1) * group)
                wr[to, at] = real[w * group : (w + 1) * group]
                wi[to, at] = imag[w * group : (w + 1) * group]

    def pick(s):
        if s == 0:
            tables[3].wait()
        owned = s * group + lax.rem(src_ref[4 * column[s] + place], group)
        for w in range(sets):
            gs[s, mine, 2 * w : 2 * w + 1, :] = wr[pl.ds(w * width + owned, 1), :]
            gs[s, mine, 2 * w + 1 : 2 * w + 2, :] = wi[pl.ds(w * width + owned, 1), :]

    def passing(s, block, target):
        mask = block ^ target
        chan, win = masked(target)
        slot = gs.at[s, slot_of(*masked(block))]
        return pltpu.make_async_remote_copy(
            src_ref=slot, dst_ref=slot, send_sem=g_send.at[s], recv_sem=g_recv.at[s, mask],
            device_id={"chan": chan, "win": win}, device_id_type=MESH,
        )

    gather = []
    for s in range(STAGES):
        moves = [passing(s, 0, target) for target in (1, 2, 4, 6, 8, 9)]
        moves += [passing(s, 8, target) for target in (2, 4, 6)]
        moves += [passing(s, block, 1) for block in (2, 4, 6, 10, 12, 14)]
        order = (1, 2, 4, 6, 8, 9, 10, 12, 14, 3, 5, 7, 11, 13, 15)
        gather.append(dict(zip(order, moves)))

    def relay(s, arrived, sent):
        for mask in arrived:
            gather[s][mask].wait_recv()
        for mask in sent:
            gather[s][mask].start()

    for s in range(STAGES):
        settle(recv.at[s], a_recv.at[s])
        normalise(s)
        transform(s)
        whiten(s)
        pick(s)
        if s == 0:
            relay(0, (), (8, 9, 1, 2, 4, 6))
    tables[2].wait()

    def compute(s, slots):
        count = len(slots)
        for t in range(tiles):
            at = slice(t * LANES, (t + 1) * LANES)
            sums = {}
            for w in range(sets):
                white = [
                    (wr[v : v + group, at], wi[v : v + group, at])
                    for v in range(w * width, (w + 1) * width, group)
                ]
                for j in range(count):
                    sr = gs[s, slots[j], 2 * w : 2 * w + 1, at]
                    si = gs[s, slots[j], 2 * w + 1 : 2 * w + 2, at]
                    for v in range(STAGES):
                        real, imag = white[v]
                        new = (sr * real + si * imag, sr * imag - si * real)
                        for k in range(2):
                            key = v, j, k
                            sums[key] = new[k] if w == 0 else sums[key] + new[k]
            for v in range(STAGES):
                for j in range(0, count, 2):
                    for k in range(2):
                        both = jnp.concatenate([sums[v, j, k], sums[v, j + 1, k]], axis=0)
                        high, low = halves(both)
                        col = k * freq + t * LANES
                        to = (v * count + j) * group
                        cc[to : to + 2 * group, col : col + LANES] = high
                        to = to + count * width
                        cc[to : to + 2 * group, col : col + LANES] = low
        half = count * width
        return folded(dot(cc[: 2 * half], lag[0])) + dot(cc[:half], lag[1])

    def deliver(q, v, owner, there, first, count, value):
        at = pl.ds(pl.multiple_of(first, 2 * group), count * group)
        here = (owner == row) & (column[v] == me)

        @pl.when(here)
        def _():
            land[upper, place, there, at] = value

        @pl.when(jnp.logical_not(here))
        def _():
            part[q, v, at] = value
            pltpu.make_async_remote_copy(
                src_ref=part.at[q, v, at], dst_ref=land.at[upper, place, there, at],
                send_sem=r_send.at[0], recv_sem=r_recv.at[0],
                device_id={"win": owner, "chan": column[v]}, device_id_type=MESH,
            ).start()

    def await_source(s, mask):
        pltpu.make_async_remote_copy(
            src_ref=gs.at[0, mine], dst_ref=gs.at[0, mine],
            send_sem=g_send.at[s], recv_sem=g_recv.at[s, mask],
            device_id={"chan": flip(core, 1) + me - core}, device_id_type=MESH,
        ).wait_recv()

    for z, mask in enumerate((1, 9)):
        if z == 1:
            relay(0, (8,), (10, 12, 14))
            relay(1, (), (8, 9, 1, 2, 4, 6))
        await_source(0, mask)
        line = flip(side, z)
        base = line * chan_count + 4 * y + 2 * x
        result = compute(0, (base, base + 1))
        for v in range(STAGES):
            value = result[2 * group * v : 2 * group * (v + 1)]
            deliver(0, v, 2 * far[0] + x, y, line * 2 * group, 2, value)

    def step(q, _):
        s, p = q // 4, lax.rem(q, 4)
        cross, later = lax.rem(p, 2), p // 2
        second = p * (3 - p) * (2 - p) // 2
        third = p * (p - 1) * (3 - p) // 2
        last = p * (p - 1) * (p - 2) // 6

        @pl.when(q == 1)
        def _():
            relay(0, (2, 6, 4), (3, 7, 5))

        @pl.when(q == 2)
        def _():
            relay(0, (12, 10), (13, 11))

        @pl.when(q == 3)
        def _():
            relay(0, (14,), (15,))
            relay(1, (8,), (10, 12, 14))

        @pl.when(q == 4)
        def _():
            relay(1, (2, 6, 4), (3, 7, 5))

        @pl.when(q == 5)
        def _():
            relay(1, (12, 10), (13, 11))

        @pl.when(q == 6)
        def _():
            relay(1, (14,), (15,))

        await_source(s, 1 + 2 * p + 4 * last)
        await_source(s, 9 - 2 * second + 4 * third + 6 * last)
        there = (1 - cross) * flip(y, later) + cross * flip(side, later)
        owner = 2 * (far[0] + s * (far[1] - far[0])) + flip(x, cross)
        slots = []
        for j in range(4):
            b, k = j // 2, j % 2
            r = (1 - cross) * b + cross * there
            at_y = (1 - cross) * there + cross * b
            slots.append(r * chan_count + 4 * at_y + 2 * flip(x, cross) + k)
        result = compute(s, slots)
        for v in range(STAGES):
            value = result[4 * group * v : 4 * group * (v + 1)]
            deliver(q, v, owner, there, 0, 4, value)
        return 0

    lax.fori_loop(1, STAGES * win_count, step, 0)

    settle(part.at[: STAGES * win_count - 1], r_recv.at[0])
    cross = side + x - 2 * side * x
    for there in range(2):
        for g in range(4):
            for j in range(4):
                b, k = j // 2, j % 2
                at = slice(j * group, (j + 1) * group)
                source = 4 * k + (1 - cross) * (2 * b + there) + cross * (b + 2 * there)
                to = pl.ds(pl.multiple_of((4 * source + g) * group, group), group)
                out_ref[to, :] = land[0, g, there, at] + land[1, g, there, at]

    for s in range(STAGES):
        settle(xt.at[s, : 2 * chan_count - 1], a_send.at[s])
        settle(gs.at[s, : 2 * chan_count - 1], g_send.at[s])
    settle(part.at[: STAGES * win_count - 1], r_send.at[0])


def fused(records, sources):
    chan_count, win_count = lax.axis_size("chan"), lax.axis_size("win")
    windows, time, channels = records.shape
    length = time * chan_count
    freq = length // 2
    group = channels // chan_count // 4
    sets = 2 * windows
    rows = sets * group
    source_count = sources.shape[0]
    lag_count = length // 4
    reach = length // 32
    half_width = min(16, time)
    owned = source_count // win_count
    factor = 1.0 / math.sqrt(windows * win_count * freq)
    fwd = forward_blocks(length, time)
    band = smooth_table(freq, reach)
    lag = lag_table(length, lag_count, factor)
    width = STAGES * group
    block = owned * 2 * width
    vmem = pl.BlockSpec(memory_space=pltpu.VMEM)
    hbm = pl.BlockSpec(memory_space=pltpu.HBM)
    dma = pltpu.SemaphoreType.DMA
    out = pl.pallas_call(
        functools.partial(fused_kernel, half_width, reach, chan_count, win_count),
        out_shape=pltpu.VMEM((block, lag_count), F32),
        in_specs=[hbm] * 5,
        out_specs=vmem,
        scratch_shapes=[
            pltpu.SMEM(sources.shape, jnp.int32),
            pltpu.VMEM(records.shape, F32),
            pltpu.VMEM((2, 2 * chan_count, windows * group, time), F32),
            pltpu.VMEM((STAGES, chan_count, 2, windows * group, time), F32),
            pltpu.VMEM((chan_count, rows, time), F32),
            pltpu.VMEM((4, 2 * rows, 2 * time), BF16),
            pltpu.VMEM((rows, freq), F32),
            pltpu.VMEM((rows, freq), F32),
            pltpu.VMEM((2 * rows, freq), BF16),
            pltpu.VMEM((sets * width, freq), F32),
            pltpu.VMEM((sets * width, freq), F32),
            pltpu.VMEM((STAGES, 2 * chan_count, 2 * sets, freq), F32),
            pltpu.VMEM((8 * width, 2 * freq), BF16),
            pltpu.VMEM((STAGES * win_count, STAGES, 4 * group, lag_count), F32),
            pltpu.VMEM((2, 4, 2, 4 * group, lag_count), F32),
            pltpu.VMEM(fwd.shape, BF16),
            pltpu.VMEM(band.shape, BF16),
            pltpu.VMEM(lag.shape, BF16),
            dma((windows,)),
            dma((4,)),
            dma((STAGES,)),
            dma((STAGES,)),
            dma((STAGES,)),
            dma((STAGES, 2 * chan_count)),
            dma((1,)),
            dma((1,)),
        ],
        compiler_params=pltpu.CompilerParams(
            collective_id=0, has_side_effects=True, vmem_limit_bytes=40_000_000
        ),
        name="interferometry",
    )(*[
        pltpu.with_memory_space_constraint(value, pltpu.HBM)
        for value in (sources, records, jnp.asarray(fwd), jnp.asarray(band), jnp.asarray(lag))
    ])
    return out.reshape(owned, 2 * width, lag_count).transpose(0, 2, 1)


def fits(records, sources):
    chan_count, win_count = lax.axis_size("chan"), lax.axis_size("win")
    windows, time, channels = records.shape
    return (
        time == LANES and chan_count == 8 and win_count == 4 and channels % LANES == 0
        and channels == 32 * chan_count and sources.shape[0] == 4 * chan_count
        and windows % 2 == 0
    )


def body(records, sources):
    return fused(records, sources) if fits(records, sources) else local(records, sources)


def solution(mesh):
    placed = (P("win", "chan", None), P())
    return jax.shard_map(
        body, mesh=mesh, in_specs=placed, out_specs=P("win", None, "chan"), check_vma=False
    )
```

time: 40.6 us -> 32.1 us (0.79)
  the two profiles are of different devices: /device:TPU:6 before, /device:TPU:0 now
where the time goes in v1:
time: 32.1 us; the launch traced here: 31.9 us
  Pallas kernels  31.2 us (97%)
  local copies, waits for them, and re-layouts  0.71 us (2%)
    pallas_call x1, Pallas kernels, fused(): pl.pallas_call(functools.partial(fused_kernel, half_width, reach, chan_co...  31.2 us
    unnamed x1, local copies, waits for them, and re-layouts  0.71 us

profile of v1, /device:TPU:0, one launch (start us, length us, event | category | flops | bytes accessed | tf_op | source)
XLA Modules:
  0.0 31.9 jit_solution(14428990868248504239)
XLA Ops:
  0.0 31.2 %interferometry.1 = f32[256,256]{1,0:T(8,128)S(1)} custom-call(s32[32]{0:T(128)} %src_hbm.1, f32[4,128,256]{2,1,0:T(8,128)} %rec_hbm.1, bf16[2,4,256,256]{3,2,1,0:T(8,128)(2,1)} %constant.6.clone.fwd_hbm, bf16[512,512]{1,0:T(8,128)(2,1)} %constant.7.clone.band_hbm, bf16[2,1024,256]{2,1,0:T(8,128)(2,1)} %constant.8.clone.lag_hbm), custom_call_target="tpu_custom_call" | custom-call | tf_op jit(solution)/shard_map/interferometry/pallas_call | solution.py:524
  31.2 0.7 %copy.7 = f32[8,256,32]{1,2,0:T(8,128)} copy(f32[8,256,32]{1,2,0:T(8,128)S(1)} %bitcast.3) | data formatting | bytes 524288

commit v2 on v1

--- a/solution.py
+++ b/solution.py
@@ -184,9 +184,9 @@
 def fused_kernel(
     half_width, smooth_reach, chan_count, win_count,
     src_hbm, rec_hbm, fwd_hbm, band_hbm, lag_hbm, out_ref,
-    src_ref, rec, xt, recv, nrm, yy, fr, fi, mm, wr, wi, gs, cc, part, land,
+    src_ref, rec, xt, recv, nrm, yy, fr, fi, mm, ww, wo, gs, cc, part, land,
     fwd, band, lag,
-    rec_sem, tab_sem, a_send, a_recv, g_send, g_recv, r_send, r_recv,
+    rec_sem, tab_sem, a_send, a_recv, g_send, g_recv, w_send, w_recv, r_send, r_recv,
 ):
     me = lax.axis_index("chan")
     row = lax.axis_index("win")
@@ -194,8 +194,7 @@
     sets = 2 * windows
     group = xt.shape[2] // windows
     rows = sets * group
-    width = STAGES * group
-    freq = wr.shape[1]
+    freq = fr.shape[1]
     tiles = freq // LANES
     core, x, y = lax.rem(me, 2), lax.rem(me // 2, 2), me // 4
     upper, side = row // 2, lax.rem(row, 2)
@@ -317,186 +316,187 @@
             at = slice(g * 256, (g + 1) * 256)
             smoothed = folded(dot(mm[...], band[:, at])) / (2 * smooth_reach + 1) + WHITE_EPSILON
             inverse = 1.0 / smoothed
-            real, imag = fr[:, at] * inverse, fi[:, at] * inverse
-            for w in range(sets):
-                to = slice(w * width + s * group, w * width + (s + 1) * group)
-                wr[to, at] = real[w * group : (w + 1) * group]
-                wi[to, at] = imag[w * group : (w + 1) * group]
+            ww[s, 0, :, at] = fr[:, at] * inverse
+            ww[s, 1, :, at] = fi[:, at] * inverse
 
     def pick(s):
         if s == 0:
             tables[3].wait()
-        owned = s * group + lax.rem(src_ref[4 * column[s] + place], group)
+        owned = lax.rem(src_ref[4 * column[s] + place], group)
         for w in range(sets):
-            gs[s, mine, 2 * w : 2 * w + 1, :] = wr[pl.ds(w * width + owned, 1), :]
-            gs[s, mine, 2 * w + 1 : 2 * w + 2, :] = wi[pl.ds(w * width + owned, 1), :]
-
-    def passing(s, block, target):
-        mask = block ^ target
-        chan, win = masked(target)
-        slot = gs.at[s, slot_of(*masked(block))]
+            for k in range(2):
+                line = 2 * w + k
+                gs[s, mine, line : line + 1, :] = ww[s, k, pl.ds(w * group + owned, 1), :]
+
+    def offer(s, mask):
+        chan, win = masked(mask)
         return pltpu.make_async_remote_copy(
-            src_ref=slot, dst_ref=slot, send_sem=g_send.at[s], recv_sem=g_recv.at[s, mask],
+            src_ref=gs.at[s, mine], dst_ref=gs.at[s, mine],
+            send_sem=g_send.at[s], recv_sem=g_recv.at[s, mask],
             device_id={"chan": chan, "win": win}, device_id_type=MESH,
         )
 
-    gather = []
-    for s in range(STAGES):
-        moves = [passing(s, 0, target) for target in (1, 2, 4, 6, 8, 9)]
-        moves += [passing(s, 8, target) for target in (2, 4, 6)]
-        moves += [passing(s, block, 1) for block in (2, 4, 6, 10, 12, 14)]
-        order = (1, 2, 4, 6, 8, 9, 10, 12, 14, 3, 5, 7, 11, 13, 15)
-        gather.append(dict(zip(order, moves)))
-
-    def relay(s, arrived, sent):
-        for mask in arrived:
-            gather[s][mask].wait_recv()
-        for mask in sent:
-            gather[s][mask].start()
+    def offers(s, masks):
+        for mask in masks:
+            offer(s, mask).start()
+
+    def arrive(s, masks):
+        for mask in masks:
+            offer(s, mask).wait_recv()
+
+    def share(s):
+        chan, win = masked(1)
+        return pltpu.make_async_remote_copy(
+            src_ref=ww.at[s], dst_ref=wo.at[s],
+            send_sem=w_send.at[s], recv_sem=w_recv.at[s],
+            device_id={"chan": chan, "win": win}, device_id_type=MESH,
+        )
 
     for s in range(STAGES):
         settle(recv.at[s], a_recv.at[s])
+        if s == 1:
+            offers(0, (6, 12, 10, 14))
         normalise(s)
         transform(s)
         whiten(s)
+        share(s).start()
         pick(s)
-        if s == 0:
-            relay(0, (), (8, 9, 1, 2, 4, 6))
+        offers(s, ((1, 2, 4, 8), (2, 4, 8))[s])
     tables[2].wait()
 
-    def compute(s, slots):
-        count = len(slots)
+    def compute(sources, entries):
+        half = len(entries) * group
+        targets = sorted({target for _, target in entries})
         for t in range(tiles):
             at = slice(t * LANES, (t + 1) * LANES)
             sums = {}
             for w in range(sets):
-                white = [
-                    (wr[v : v + group, at], wi[v : v + group, at])
-                    for v in range(w * width, (w + 1) * width, group)
+                rows_at = slice(w * group, (w + 1) * group)
+                white = {
+                    (j, v): tuple((ww, wo)[j][v, k, rows_at, at] for k in range(2))
+                    for j, v in targets
+                }
+                lines = [
+                    (gs[s, slot, 2 * w : 2 * w + 1, at], gs[s, slot, 2 * w + 1 : 2 * w + 2, at])
+                    for s, slot in sources
                 ]
-                for j in range(count):
-                    sr = gs[s, slots[j], 2 * w : 2 * w + 1, at]
-                    si = gs[s, slots[j], 2 * w + 1 : 2 * w + 2, at]
-                    for v in range(STAGES):
-                        real, imag = white[v]
-                        new = (sr * real + si * imag, sr * imag - si * real)
-                        for k in range(2):
-                            key = v, j, k
-                            sums[key] = new[k] if w == 0 else sums[key] + new[k]
-            for v in range(STAGES):
-                for j in range(0, count, 2):
+                for n, (source, target) in enumerate(entries):
+                    (sr, si), (real, imag) = lines[source], white[target]
+                    new = (sr * real + si * imag, sr * imag - si * real)
                     for k in range(2):
-                        both = jnp.concatenate([sums[v, j, k], sums[v, j + 1, k]], axis=0)
-                        high, low = halves(both)
-                        col = k * freq + t * LANES
-                        to = (v * count + j) * group
-                        cc[to : to + 2 * group, col : col + LANES] = high
-                        to = to + count * width
-                        cc[to : to + 2 * group, col : col + LANES] = low
-        half = count * width
+                        sums[n, k] = new[k] if w == 0 else sums[n, k] + new[k]
+            for n in range(0, len(entries), 2):
+                for k in range(2):
+                    high, low = halves(jnp.concatenate([sums[n, k], sums[n + 1, k]], axis=0))
+                    col = k * freq + t * LANES
+                    cc[n * group : (n + 2) * group, col : col + LANES] = high
+                    cc[half + n * group : half + (n + 2) * group, col : col + LANES] = low
         return folded(dot(cc[: 2 * half], lag[0])) + dot(cc[:half], lag[1])
 
-    def deliver(q, v, owner, there, first, count, value):
-        at = pl.ds(pl.multiple_of(first, 2 * group), count * group)
+    def deliver(staged, landed, j, v, owner, value):
+        def send():
+            staged[...] = value
+            pltpu.make_async_remote_copy(
+                src_ref=staged, dst_ref=landed, send_sem=r_send.at[0], recv_sem=r_recv.at[0],
+                device_id={"win": owner, "chan": column[v] + j * (1 - 2 * core)},
+                device_id_type=MESH,
+            ).start()
+
+        if j == 1:
+            send()
+            return
         here = (owner == row) & (column[v] == me)
 
         @pl.when(here)
         def _():
-            land[upper, place, there, at] = value
+            landed[...] = value
 
         @pl.when(jnp.logical_not(here))
         def _():
-            part[q, v, at] = value
+            send()
+
+    steps = 2 * win_count - 1
+    base = side * chan_count + 4 * y + 2 * x
+    arrive(0, (1,))
+    entries = [(k, (0, v)) for v in range(STAGES) for k in range(2)]
+    result = compute([(0, base), (0, base + 1)], entries)
+    for n, (k, (_, v)) in enumerate(entries):
+        at = slice(n * group, (n + 1) * group)
+        spot = pl.ds(pl.multiple_of(y * group, group), group)
+        deliver(
+            part.at[2 * steps, at], land.at[upper, place, side, k, spot], 0, v,
+            2 * far[0] + x, result[at],
+        )
+    offers(1, (6,))
+    for s in range(STAGES):
+        share(s).wait_recv()
+    arrive(0, (4,))
+    entries = [(0, (j, v)) for j in range(2) for v in range(STAGES)]
+    result = compute([(0, side * chan_count + 4 * (1 - y) + 2 * x + core)], entries)
+    for n, (_, (j, v)) in enumerate(entries):
+        at = slice(n * group, (n + 1) * group)
+        spot = pl.ds(pl.multiple_of((1 - y) * group, group), group)
+        deliver(
+            part.at[2 * steps + 2, at], land.at[upper, place, side, core, spot], j, v,
+            2 * far[0] + x, result[at],
+        )
+
+    def forward():
+        arrive(1, (8,))
+        for target in (2, 4, 6):
+            chan, win = masked(target)
+            slot = gs.at[1, slot_of(*masked(8))]
             pltpu.make_async_remote_copy(
-                src_ref=part.at[q, v, at], dst_ref=land.at[upper, place, there, at],
-                send_sem=r_send.at[0], recv_sem=r_recv.at[0],
-                device_id={"win": owner, "chan": column[v]}, device_id_type=MESH,
+                src_ref=slot, dst_ref=slot, send_sem=g_send.at[1], recv_sem=g_recv.at[1, 8 | target],
+                device_id={"chan": chan, "win": win}, device_id_type=MESH,
             ).start()
 
-    def await_source(s, mask):
-        pltpu.make_async_remote_copy(
-            src_ref=gs.at[0, mine], dst_ref=gs.at[0, mine],
-            send_sem=g_send.at[s], recv_sem=g_recv.at[s, mask],
-            device_id={"chan": flip(core, 1) + me - core}, device_id_type=MESH,
-        ).wait_recv()
-
-    for z, mask in enumerate((1, 9)):
-        if z == 1:
-            relay(0, (8,), (10, 12, 14))
-            relay(1, (), (8, 9, 1, 2, 4, 6))
-        await_source(0, mask)
-        line = flip(side, z)
-        base = line * chan_count + 4 * y + 2 * x
-        result = compute(0, (base, base + 1))
-        for v in range(STAGES):
-            value = result[2 * group * v : 2 * group * (v + 1)]
-            deliver(0, v, 2 * far[0] + x, y, line * 2 * group, 2, value)
-
     def step(q, _):
-        s, p = q // 4, lax.rem(q, 4)
-        cross, later = lax.rem(p, 2), p // 2
-        second = p * (3 - p) * (2 - p) // 2
-        third = p * (p - 1) * (3 - p) // 2
-        last = p * (p - 1) * (p - 2) // 6
-
+        s = (q + 1) // 4
+        i = q - 3 * s
+        e = flip(x, 1 - upper)
+        early = (2 - i) * (1 - i) // 2 * (2 - e) + i * (2 - i) * (1 + 2 * e) + i * (i - 1) // 2 * (3 - e)
+        t = (1 - s) * early + s * (2 * lax.rem(i, 2) + flip(i // 2, flip(x, upper)))
+        at_x, r = flip(x, lax.rem(t, 2)), flip(side, t // 2)
+        owner = 2 * (far[0] + s * (far[1] - far[0])) + at_x
         @pl.when(q == 1)
         def _():
-            relay(0, (2, 6, 4), (3, 7, 5))
-
-        @pl.when(q == 2)
-        def _():
-            relay(0, (12, 10), (13, 11))
-
-        @pl.when(q == 3)
-        def _():
-            relay(0, (14,), (15,))
-            relay(1, (8,), (10, 12, 14))
-
-        @pl.when(q == 4)
-        def _():
-            relay(1, (2, 6, 4), (3, 7, 5))
-
-        @pl.when(q == 5)
-        def _():
-            relay(1, (12, 10), (13, 11))
-
-        @pl.when(q == 6)
-        def _():
-            relay(1, (14,), (15,))
-
-        await_source(s, 1 + 2 * p + 4 * last)
-        await_source(s, 9 - 2 * second + 4 * third + 6 * last)
-        there = (1 - cross) * flip(y, later) + cross * flip(side, later)
-        owner = 2 * (far[0] + s * (far[1] - far[0])) + flip(x, cross)
-        slots = []
-        for j in range(4):
-            b, k = j // 2, j % 2
-            r = (1 - cross) * b + cross * there
-            at_y = (1 - cross) * there + cross * b
-            slots.append(r * chan_count + 4 * at_y + 2 * flip(x, cross) + k)
-        result = compute(s, slots)
-        for v in range(STAGES):
-            value = result[4 * group * v : 4 * group * (v + 1)]
-            deliver(q, v, owner, there, 0, 4, value)
+            forward()
+
+        for k, masks in enumerate(((4,), (2, 6), (8, 12), (10, 14))):
+            for stage in range(1 - min(k, 1), STAGES):
+                @pl.when((s == stage) & (t == k))
+                def _():
+                    arrive(stage, masks[stage:] if k == 2 else masks)
+
+        slots = [(s, r * chan_count + 4 * there + 2 * at_x + core) for there in range(2)]
+        entries = [(n, (j, v)) for j in range(2) for v in range(STAGES) for n in range(2)]
+        result = compute(slots, entries)
+        for j in (1, 0):
+            for v in range(STAGES):
+                first = (2 * j + v) * 2 * group
+                deliver(
+                    part.at[2 * q + j, v * 2 * group : (v + 1) * 2 * group],
+                    land.at[upper, place, r, core], j, v, owner, result[first : first + 2 * group],
+                )
         return 0
 
-    lax.fori_loop(1, STAGES * win_count, step, 0)
-
-    settle(part.at[: STAGES * win_count - 1], r_recv.at[0])
-    cross = side + x - 2 * side * x
-    for there in range(2):
-        for g in range(4):
-            for j in range(4):
-                b, k = j // 2, j % 2
-                at = slice(j * group, (j + 1) * group)
-                source = 4 * k + (1 - cross) * (2 * b + there) + cross * (b + 2 * there)
-                to = pl.ds(pl.multiple_of((4 * source + g) * group, group), group)
-                out_ref[to, :] = land[0, g, there, at] + land[1, g, there, at]
+    lax.fori_loop(0, steps, step, 0)
+
+    settle(part.at[: 2 * steps + 1], r_recv.at[0])
+    for g in range(4):
+        for r in range(2):
+            for k in range(2):
+                for there in range(2):
+                    at = slice(there * group, (there + 1) * group)
+                    to = ((4 * k + 2 * r + there) * 4 + g) * group
+                    out_ref[to : to + group, :] = land[0, g, r, k, at] + land[1, g, r, k, at]
 
     for s in range(STAGES):
         settle(xt.at[s, : 2 * chan_count - 1], a_send.at[s])
-        settle(gs.at[s, : 2 * chan_count - 1], g_send.at[s])
-    settle(part.at[: STAGES * win_count - 1], r_send.at[0])
+        settle(gs.at[s, : 8 - s], g_send.at[s])
+        settle(ww.at[s], w_send.at[s])
+    settle(part.at[: 2 * steps + 1], r_send.at[0])
 
 
 def fused(records, sources):
@@ -536,12 +536,12 @@
             pltpu.VMEM((rows, freq), F32),
             pltpu.VMEM((rows, freq), F32),
             pltpu.VMEM((2 * rows, freq), BF16),
-            pltpu.VMEM((sets * width, freq), F32),
-            pltpu.VMEM((sets * width, freq), F32),
+            pltpu.VMEM((STAGES, 2, rows, freq), F32),
+            pltpu.VMEM((STAGES, 2, rows, freq), F32),
             pltpu.VMEM((STAGES, 2 * chan_count, 2 * sets, freq), F32),
-            pltpu.VMEM((8 * width, 2 * freq), BF16),
-            pltpu.VMEM((STAGES * win_count, STAGES, 4 * group, lag_count), F32),
-            pltpu.VMEM((2, 4, 2, 4 * group, lag_count), F32),
+            pltpu.VMEM((16 * group, 2 * freq), BF16),
+            pltpu.VMEM((4 * win_count + 2, 4 * group, lag_count), F32),
+            pltpu.VMEM((2, 4, 2, 2, 2 * group, lag_count), F32),
             pltpu.VMEM(fwd.shape, BF16),
             pltpu.VMEM(band.shape, BF16),
             pltpu.VMEM(lag.shape, BF16),
@@ -551,6 +551,8 @@
             dma((STAGES,)),
             dma((STAGES,)),
             dma((STAGES, 2 * chan_count)),
+            dma((STAGES,)),
+            dma((STAGES,)),
             dma((1,)),
             dma((1,)),
         ],

time: 32.1 us -> 29.3 us (0.913)
  Pallas kernels: 31.2 us -> 28.4 us
    pallas_call x1, Pallas kernels: 31.2 us -> 28.4 us  [fused(): pl.pallas_call(functools.partial(fused_kernel, half_width, reach, chan_co...]
where the time goes in v2:
time: 29.3 us; the launch traced here: 29.1 us
  Pallas kernels  28.4 us (97%)
  local copies, waits for them, and re-layouts  0.71 us (2%)
    pallas_call x1, Pallas kernels, fused(): pl.pallas_call(functools.partial(fused_kernel, half_width, reach, chan_co...  28.4 us
    unnamed x1, local copies, waits for them, and re-layouts  0.71 us

profile of v2, /device:TPU:0, one launch (start us, length us, event | category | flops | bytes accessed | tf_op | source)
XLA Modules:
  0.0 29.1 jit_solution(441965208527616335)
XLA Ops:
  0.0 28.4 %interferometry.1 = f32[256,256]{1,0:T(8,128)S(1)} custom-call(s32[32]{0:T(128)} %src_hbm.1, f32[4,128,256]{2,1,0:T(8,128)} %rec_hbm.1, bf16[2,4,256,256]{3,2,1,0:T(8,128)(2,1)} %constant.6.clone.fwd_hbm, bf16[512,512]{1,0:T(8,128)(2,1)} %constant.7.clone.band_hbm, bf16[2,1024,256]{2,1,0:T(8,128)(2,1)} %constant.8.clone.lag_hbm), custom_call_target="tpu_custom_call" | custom-call | tf_op jit(solution)/shard_map/interferometry/pallas_call | solution.py:524
  28.4 0.7 %copy.7 = f32[8,256,32]{1,2,0:T(8,128)} copy(f32[8,256,32]{1,2,0:T(8,128)S(1)} %bitcast.3) | data formatting | bytes 524288

commit v3 on v2

--- a/solution.py
+++ b/solution.py
@@ -186,7 +186,7 @@
     src_hbm, rec_hbm, fwd_hbm, band_hbm, lag_hbm, out_ref,
     src_ref, rec, xt, recv, nrm, yy, fr, fi, mm, ww, wo, gs, cc, part, land,
     fwd, band, lag,
-    rec_sem, tab_sem, a_send, a_recv, g_send, g_recv, w_send, w_recv, r_send, r_recv,
+    rec_sem, tab_sem, sent, a_recv, g_recv, w_recv, r_recv,
 ):
     me = lax.axis_index("chan")
     row = lax.axis_index("win")
@@ -255,7 +255,7 @@
             chan, win = masked(mask)
             pltpu.make_async_remote_copy(
                 src_ref=xt.at[far[s], slot_of(chan, win)], dst_ref=recv.at[s, me, side],
-                send_sem=a_send.at[s], recv_sem=a_recv.at[s],
+                send_sem=sent.at[0], recv_sem=a_recv.at[s],
                 device_id={"chan": chan, "win": win}, device_id_type=MESH,
             ).start()
         pltpu.make_async_copy(xt.at[far[s], mine], recv.at[s, me, side], a_recv.at[s]).start()
@@ -298,7 +298,8 @@
         return 0
 
     def transform(s):
-        lax.fori_loop(0, rows // 16, butterfly, 0)
+        for block in range(rows // 16):
+            butterfly(block, 0)
         if s == 0:
             tables[0].wait()
         for g in range(4):
@@ -332,7 +333,7 @@
         chan, win = masked(mask)
         return pltpu.make_async_remote_copy(
             src_ref=gs.at[s, mine], dst_ref=gs.at[s, mine],
-            send_sem=g_send.at[s], recv_sem=g_recv.at[s, mask],
+            send_sem=sent.at[1], recv_sem=g_recv.at[s, mask // 2],
             device_id={"chan": chan, "win": win}, device_id_type=MESH,
         )
 
@@ -348,7 +349,7 @@
         chan, win = masked(1)
         return pltpu.make_async_remote_copy(
             src_ref=ww.at[s], dst_ref=wo.at[s],
-            send_sem=w_send.at[s], recv_sem=w_recv.at[s],
+            send_sem=sent.at[2], recv_sem=w_recv.at[0],
             device_id={"chan": chan, "win": win}, device_id_type=MESH,
         )
 
@@ -397,7 +398,7 @@
         def send():
             staged[...] = value
             pltpu.make_async_remote_copy(
-                src_ref=staged, dst_ref=landed, send_sem=r_send.at[0], recv_sem=r_recv.at[0],
+                src_ref=staged, dst_ref=landed, send_sem=sent.at[3], recv_sem=r_recv.at[0],
                 device_id={"win": owner, "chan": column[v] + j * (1 - 2 * core)},
                 device_id_type=MESH,
             ).start()
@@ -428,8 +429,7 @@
             2 * far[0] + x, result[at],
         )
     offers(1, (6,))
-    for s in range(STAGES):
-        share(s).wait_recv()
+    settle(wo, w_recv.at[0])
     arrive(0, (4,))
     entries = [(0, (j, v)) for j in range(2) for v in range(STAGES)]
     result = compute([(0, side * chan_count + 4 * (1 - y) + 2 * x + core)], entries)
@@ -447,7 +447,7 @@
             chan, win = masked(target)
             slot = gs.at[1, slot_of(*masked(8))]
             pltpu.make_async_remote_copy(
-                src_ref=slot, dst_ref=slot, send_sem=g_send.at[1], recv_sem=g_recv.at[1, 8 | target],
+                src_ref=slot, dst_ref=slot, send_sem=sent.at[1], recv_sem=g_recv.at[1, 4 + target // 2],
                 device_id={"chan": chan, "win": win}, device_id_type=MESH,
             ).start()
 
@@ -492,11 +492,10 @@
                     to = ((4 * k + 2 * r + there) * 4 + g) * group
                     out_ref[to : to + group, :] = land[0, g, r, k, at] + land[1, g, r, k, at]
 
-    for s in range(STAGES):
-        settle(xt.at[s, : 2 * chan_count - 1], a_send.at[s])
-        settle(gs.at[s, : 8 - s], g_send.at[s])
-        settle(ww.at[s], w_send.at[s])
-    settle(part.at[: 2 * steps + 1], r_send.at[0])
+    settle(part.at[: 2 * steps + 1], sent.at[0])
+    settle(gs.at[0, : 2 * chan_count - 1], sent.at[1])
+    settle(ww, sent.at[2])
+    settle(part.at[: 2 * steps + 1], sent.at[3])
 
 
 def fused(records, sources):
@@ -547,12 +546,9 @@
             pltpu.VMEM(lag.shape, BF16),
             dma((windows,)),
             dma((4,)),
+            dma((4,)),
             dma((STAGES,)),
-            dma((STAGES,)),
-            dma((STAGES,)),
-            dma((STAGES, 2 * chan_count)),
-            dma((STAGES,)),
-            dma((STAGES,)),
+            dma((STAGES, chan_count)),
             dma((1,)),
             dma((1,)),
         ],

time: 29.3 us -> 29 us (0.990)
  Pallas kernels: 28.4 us -> 28.1 us
where the time goes in v3:
time: 29 us; the launch traced here: 28.9 us
  Pallas kernels  28.1 us (97%)
  local copies, waits for them, and re-layouts  0.71 us (2%)
    pallas_call x1, Pallas kernels, fused(): pl.pallas_call(functools.partial(fused_kernel, half_width, reach, chan_co...  28.1 us
    unnamed x1, local copies, waits for them, and re-layouts  0.71 us

profile of v3, /device:TPU:0, one launch (start us, length us, event | category | flops | bytes accessed | tf_op | source)
XLA Modules:
  0.0 28.9 jit_solution(7614965051784274424)
XLA Ops:
  0.0 28.1 %interferometry.1 = f32[256,256]{1,0:T(8,128)S(1)} custom-call(s32[32]{0:T(128)} %src_hbm.1, f32[4,128,256]{2,1,0:T(8,128)} %rec_hbm.1, bf16[2,4,256,256]{3,2,1,0:T(8,128)(2,1)} %constant.6.clone.fwd_hbm, bf16[512,512]{1,0:T(8,128)(2,1)} %constant.7.clone.band_hbm, bf16[2,1024,256]{2,1,0:T(8,128)(2,1)} %constant.8.clone.lag_hbm), custom_call_target="tpu_custom_call" | custom-call | tf_op jit(solution)/shard_map/interferometry/pallas_call | solution.py:523
  28.2 0.7 %copy.7 = f32[8,256,32]{1,2,0:T(8,128)} copy(f32[8,256,32]{1,2,0:T(8,128)S(1)} %bitcast.3) | data formatting | bytes 524288

commit v4 on v3

--- a/solution.py
+++ b/solution.py
@@ -362,7 +362,7 @@
         whiten(s)
         share(s).start()
         pick(s)
-        offers(s, ((1, 2, 4, 8), (2, 4, 8))[s])
+        offers(s, ((1, 2, 4, 8), (8,))[s])
     tables[2].wait()
 
     def compute(sources, entries):
@@ -428,7 +428,7 @@
             part.at[2 * steps, at], land.at[upper, place, side, k, spot], 0, v,
             2 * far[0] + x, result[at],
         )
-    offers(1, (6,))
+    offers(1, (2, 4, 6))
     settle(wo, w_recv.at[0])
     arrive(0, (4,))
     entries = [(0, (j, v)) for j in range(2) for v in range(STAGES)]
@@ -456,7 +456,7 @@
         i = q - 3 * s
         e = flip(x, 1 - upper)
         early = (2 - i) * (1 - i) // 2 * (2 - e) + i * (2 - i) * (1 + 2 * e) + i * (i - 1) // 2 * (3 - e)
-        t = (1 - s) * early + s * (2 * lax.rem(i, 2) + flip(i // 2, flip(x, upper)))
+        t = (1 - s) * early + s * ((side + upper - 2 * side * upper) * (2 * lax.rem(i, 2) + flip(i // 2, flip(x, upper))) + (1 - (side + upper - 2 * side * upper)) * (2 * (i // 2) + flip(lax.rem(i, 2), flip(x, upper))))
         at_x, r = flip(x, lax.rem(t, 2)), flip(side, t // 2)
         owner = 2 * (far[0] + s * (far[1] - far[0])) + at_x
         @pl.when(q == 1)

time: 29 us -> 29 us (level)
  no operation moved by 1% of the time
where the time goes in v4:
time: 29 us; the launch traced here: 28.9 us
  Pallas kernels  28.1 us (97%)
  local copies, waits for them, and re-layouts  0.71 us (2%)
    pallas_call x1, Pallas kernels, fused(): pl.pallas_call(functools.partial(fused_kernel, half_width, reach, chan_co...  28.1 us
    unnamed x1, local copies, waits for them, and re-layouts  0.71 us

profile of v4, /device:TPU:0, one launch (start us, length us, event | category | flops | bytes accessed | tf_op | source)
XLA Modules:
  0.0 28.9 jit_solution(2076475682961362611)
XLA Ops:
  0.0 28.1 %interferometry.1 = f32[256,256]{1,0:T(8,128)S(1)} custom-call(s32[32]{0:T(128)} %src_hbm.1, f32[4,128,256]{2,1,0:T(8,128)} %rec_hbm.1, bf16[2,4,256,256]{3,2,1,0:T(8,128)(2,1)} %constant.6.clone.fwd_hbm, bf16[512,512]{1,0:T(8,128)(2,1)} %constant.7.clone.band_hbm, bf16[2,1024,256]{2,1,0:T(8,128)(2,1)} %constant.8.clone.lag_hbm), custom_call_target="tpu_custom_call" | custom-call | tf_op jit(solution)/shard_map/interferometry/pallas_call | solution.py:523
  28.2 0.7 %copy.7 = f32[8,256,32]{1,2,0:T(8,128)} copy(f32[8,256,32]{1,2,0:T(8,128)S(1)} %bitcast.3) | data formatting | bytes 524288

commit v5 on v4

--- a/solution.py
+++ b/solution.py
@@ -251,7 +251,7 @@
     pl.semaphore_wait(barrier, 2 * chan_count - 1 + 2 * STAGES)
 
     for s in range(STAGES):
-        for mask in (14, 15, 12, 13, 10, 11, 6, 7, 8, 9, 4, 5, 2, 3, 1):
+        for mask in ((14, 15, 12, 13, 10, 11, 6, 7, 8, 9, 4, 5, 2, 3, 1), (15, 14, 13, 12, 11, 10, 7, 6, 9, 8, 5, 4, 3, 2, 1))[s]:
             chan, win = masked(mask)
             pltpu.make_async_remote_copy(
                 src_ref=xt.at[far[s], slot_of(chan, win)], dst_ref=recv.at[s, me, side],

time: 29 us -> 28.6 us (0.986)
  Pallas kernels: 28.1 us -> 27.8 us
    pallas_call x1, Pallas kernels: 28.1 us -> 27.8 us  [fused(): pl.pallas_call(functools.partial(fused_kernel, half_width, reach, chan_co...]
where the time goes in v5:
time: 28.6 us; the launch traced here: 28.5 us
  Pallas kernels  27.8 us (97%)
  local copies, waits for them, and re-layouts  0.71 us (2%)
    pallas_call x1, Pallas kernels, fused(): pl.pallas_call(functools.partial(fused_kernel, half_width, reach, chan_co...  27.8 us
    unnamed x1, local copies, waits for them, and re-layouts  0.71 us

profile of v5, /device:TPU:0, one launch (start us, length us, event | category | flops | bytes accessed | tf_op | source)
XLA Modules:
  0.0 28.5 jit_solution(15088598385837037976)
XLA Ops:
  0.0 27.8 %interferometry.1 = f32[256,256]{1,0:T(8,128)S(1)} custom-call(s32[32]{0:T(128)} %src_hbm.1, f32[4,128,256]{2,1,0:T(8,128)} %rec_hbm.1, bf16[2,4,256,256]{3,2,1,0:T(8,128)(2,1)} %constant.6.clone.fwd_hbm, bf16[512,512]{1,0:T(8,128)(2,1)} %constant.7.clone.band_hbm, bf16[2,1024,256]{2,1,0:T(8,128)(2,1)} %constant.8.clone.lag_hbm), custom_call_target="tpu_custom_call" | custom-call | tf_op jit(solution)/shard_map/interferometry/pallas_call | solution.py:523
  27.8 0.7 %copy.7 = f32[8,256,32]{1,2,0:T(8,128)} copy(f32[8,256,32]{1,2,0:T(8,128)S(1)} %bitcast.3) | data formatting | bytes 524288

commit v6 on v5

--- a/solution.py
+++ b/solution.py
@@ -251,7 +251,7 @@
     pl.semaphore_wait(barrier, 2 * chan_count - 1 + 2 * STAGES)
 
     for s in range(STAGES):
-        for mask in ((14, 15, 12, 13, 10, 11, 6, 7, 8, 9, 4, 5, 2, 3, 1), (15, 14, 13, 12, 11, 10, 7, 6, 9, 8, 5, 4, 3, 2, 1))[s]:
+        for mask in ((14, 15, 12, 13, 10, 11, 6, 7, 8, 9, 4, 5, 2, 3, 1), (15, 14, 13, 12, 11, 10, 9, 8, 7, 6, 5, 4, 3, 2, 1))[s]:
             chan, win = masked(mask)
             pltpu.make_async_remote_copy(
                 src_ref=xt.at[far[s], slot_of(chan, win)], dst_ref=recv.at[s, me, side],

time: 28.6 us -> 28.6 us (level)
  no operation moved by 1% of the time
where the time goes in v6:
time: 28.6 us; the launch traced here: 28.5 us
  Pallas kernels  27.8 us (97%)
  local copies, waits for them, and re-layouts  0.71 us (2%)
    pallas_call x1, Pallas kernels, fused(): pl.pallas_call(functools.partial(fused_kernel, half_width, reach, chan_co...  27.8 us
    unnamed x1, local copies, waits for them, and re-layouts  0.71 us

profile of v6, /device:TPU:0, one launch (start us, length us, event | category | flops | bytes accessed | tf_op | source)
XLA Modules:
  0.0 28.5 jit_solution(5337981562464859293)
XLA Ops:
  0.0 27.8 %interferometry.1 = f32[256,256]{1,0:T(8,128)S(1)} custom-call(s32[32]{0:T(128)} %src_hbm.1, f32[4,128,256]{2,1,0:T(8,128)} %rec_hbm.1, bf16[2,4,256,256]{3,2,1,0:T(8,128)(2,1)} %constant.6.clone.fwd_hbm, bf16[512,512]{1,0:T(8,128)(2,1)} %constant.7.clone.band_hbm, bf16[2,1024,256]{2,1,0:T(8,128)(2,1)} %constant.8.clone.lag_hbm), custom_call_target="tpu_custom_call" | custom-call | tf_op jit(solution)/shard_map/interferometry/pallas_call | solution.py:523
  27.8 0.7 %copy.7 = f32[8,256,32]{1,2,0:T(8,128)} copy(f32[8,256,32]{1,2,0:T(8,128)S(1)} %bitcast.3) | data formatting | bytes 524288
